TPU v7x, 128 devices: a whole 4x4x4 slice. The times are simulated.
128 devices in a mesh: stream: 16 (over z, y), passage: 4 (over x_hi, core), span: 2 (over x_lo).
Axes of the slice: x: 4 (x_hi: 2, x_lo: 2; x = x_hi * 2 + x_lo), y: 4, z: 4, core: 2. Of those that a mesh axis runs over, the one named last changes fastest.
Arguments:
- residual: float32 [6, 32, 256, 256], P(None, 'stream', 'passage', 'span'), may hold values from -4 to 4
- dq_old: float32 [6, 32, 256, 256], P(None, 'stream', 'passage', 'span'), may hold values from -6 to 6
- lateral_coef: float32 [32, 256, 256], P('stream', 'passage', 'span'), may hold values from 0.05 to 0.25
- diag_inverse: float32 [6, 6, 32, 256, 256], P(None, None, 'stream', 'passage', 'span'), may hold values from -1 to 1.2, as said below
- match_list: int32 [16, 256], P('stream', 'passage'), may hold values from 0 to 255, as said below
- slide_weight: float32 [256], P('passage'), may hold values from 0 to 1
Outputs:
- dq_new: float32 [6, 32, 256, 256], P(None, 'stream', 'passage', 'span')
Inputs may be any that keep to these rules, and one draw needn't show every extreme that they name: match_list[b, p] = (p + offset_b) mod 256, where offset_b = (offset_0 + b * 64) mod 256. `diag_inverse`: each 6x6 block is a diagonal scaling of the identity plus a small antisymmetric part.
All inputs are finite; a program needn't handle non-finite values.
Results may differ from a plain program's by a relative error of at most 0.00013.
Values sent between devices are 32-bit elements; how exact they have to be, the bound alone decides.
No kernel may reach another device: no remote copies, remote signals or barrier semaphores. Data moves between devices by JAX's collectives and lax.ppermute only.
A program may use at most 320 MiB of HBM per device.

v0:
```python
import jax
import jax.numpy as jnp
from jax import lax
from jax.experimental import pallas as pl
from jax.experimental.pallas import tpu as pltpu
from jax.sharding import PartitionSpec as P

VARS = 6
PAIRS = [(a, b) for a in range(VARS) for b in range(a + 1, VARS)]
COEFS = VARS + len(PAIRS)
PLANES = 2
FORM = PLANES * COEFS
SOURCE = FORM + 1
TERM = SOURCE + PLANES * VARS
SENT = TERM + VARS
LANES = 128
PART = 4
EDGE_ROWS = 16


def vmem():
    return pl.BlockSpec(memory_space=pltpu.VMEM)


def edges_kernel(dq_ref, rows_ref):
    height = dq_ref.shape[2]
    for v in range(VARS):
        rows_ref[height * v : height * (v + 1)] = dq_ref[v, 1]
    edge = height * VARS
    rows_ref[edge:] = jnp.zeros((EDGE_ROWS, LANES), jnp.float32)
    for v in range(VARS):
        rows_ref[edge + 2 * v : edge + 2 * v + 1] = dq_ref[v, 0, 0:1]
        rows_ref[edge + 2 * v + 1 : edge + 2 * v + 2] = dq_ref[v, 0, height - 1 : height]


def columns_kernel(dq_ref, cols_ref):
    span = lax.axis_index("span")
    height = dq_ref.shape[2]
    lane = lax.broadcasted_iota(jnp.int32, (height, LANES), 1)
    cols = jnp.zeros((height, LANES), jnp.float32)
    for i in range(VARS * PLANES):
        shift = i + 2 - 2 * span
        plane = dq_ref[i // PLANES, i % PLANES]
        cols = jnp.where(lane == i + 1 - span, pltpu.roll(plane, shift, 1), cols)
    cols_ref[...] = cols.T[0:16]


def pack_kernel(d_ref, out_ref):
    def put(t, index, value):
        out_ref[2 * t, index] = value[0:PART]
        out_ref[2 * t + 1, index] = value[PART:8]

    for t in range(d_ref.shape[3] // 8):
        blocks = [
            [[d_ref[a, b, p, 8 * t : 8 * t + 8] for b in range(VARS)] for a in range(VARS)]
            for p in range(PLANES)
        ]
        off_row = off_none = off_col = jnp.zeros((8, LANES), jnp.float32)
        for d in blocks:
            for a, b in PAIRS:
                off_row += jnp.abs(d[a][b] * d[b][b] + d[b][a] * d[a][a])
                off_none += jnp.abs(d[a][b] + d[b][a])
                off_col += jnp.abs(d[a][b] * d[a][a] + d[b][a] * d[b][b])
        is_row = (off_row <= off_none) & (off_row <= off_col)
        is_none = off_none <= off_col
        put(t, FORM, jnp.where(is_row, 0.0, jnp.where(is_none, 1.0, 2.0)))
        for p, d in enumerate(blocks):
            s = [d[a][a] for a in range(VARS)]
            size = [jnp.abs(x) for x in s]
            inv = [jnp.where(x == 0.0, 0.0, 1.0 / x) for x in s]
            for a in range(VARS):
                put(t, p * COEFS + a, s[a])
            for i, (a, b) in enumerate(PAIRS):
                larger = size[a] >= size[b]
                row = jnp.where(larger, d[a][b] * inv[a], -d[b][a] * inv[b])
                col = jnp.where(larger, -d[b][a] * inv[a], d[a][b] * inv[b])
                value = jnp.where(is_row, row, jnp.where(is_none, d[a][b], col))
                put(t, p * COEFS + VARS + i, value)


def local_kernel(dq_ref, res_ref, coef_ref, core_ref, out_ref):
    odd = lax.rem(lax.axis_index("passage"), 2) == 1
    height = dq_ref.shape[2]
    sub = lax.broadcasted_iota(jnp.int32, (height, LANES), 0)
    lane = lax.broadcasted_iota(jnp.int32, (height, LANES), 1)
    for v in range(VARS):
        for p in range(PLANES):
            x = dq_ref[v, p]
            last, first = edge_rows(v, p, height)
            above = jnp.where(odd, core_ref[last : last + 1], 0.0)
            below = jnp.where(odd, 0.0, core_ref[first : first + 1])
            up = jnp.where(sub == 0, above, pltpu.roll(x, 1, 0))
            down = jnp.where(sub == height - 1, below, pltpu.roll(x, height - 1, 0))
            left = jnp.where(lane == 0, 0.0, pltpu.roll(x, 1, 1))
            right = jnp.where(lane == LANES - 1, 0.0, pltpu.roll(x, LANES - 1, 1))
            out_ref[v, p] = res_ref[v, p] - coef_ref[p] * (up + down + (left + right))


def edge_rows(v, plane, height):
    if plane:
        return height * (v + 1) - 1, height * v
    return height * VARS + 2 * v + 1, height * VARS + 2 * v


def source_kernel(
    match_ref, dq_ref, local_ref, coef_ref, weight_ref, core_ref, far_ref, cross_ref, cols_ref, _, out_ref, src, ring, sems
):
    q, span = lax.axis_index("passage"), lax.axis_index("span")
    height = dq_ref.shape[2]
    start = lax.rem(match_ref[0, 0] + 64, 256)
    tile, offset = start // 64, lax.rem(start, 64)
    odd = lax.rem(q, 2) == 1
    sub = lax.broadcasted_iota(jnp.int32, (height, LANES), 0)
    lane = lax.broadcasted_iota(jnp.int32, (height, LANES), 1)
    beyond = sub == jnp.where(odd, height - 1, 0)
    edge = lane == jnp.where(span == 0, LANES - 1, 0)
    weight = jnp.broadcast_to(weight_ref[...], (LANES, height)).T
    cols = jnp.concatenate([cols_ref[...], jnp.zeros((LANES - 16, height), jnp.float32)], 0).T

    def pick(index, v):
        way = jnp.bitwise_xor(index, q)
        face = slice(height * v, height * (v + 1))
        near = jnp.where(way == 0, dq_ref[v, 1], core_ref[face])
        away = jnp.where(way == 2, far_ref[face], cross_ref[face])
        return jnp.where(way < 2, near, away)

    def put(index, value):
        for t in range(height // PART):
            src[t, index] = value[PART * t : PART * t + PART]

    for v in range(VARS):
        for p in range(PLANES):
            last, first = edge_rows(v, p, height)
            row = jnp.where(odd, cross_ref[first : first + 1], cross_ref[last : last + 1])
            i = v * PLANES + p
            side = pltpu.roll(cols, LANES - 1 - i, 1)
            rest = jnp.where(beyond, row, 0.0) + jnp.where(edge, side, 0.0)
            put(p * VARS + v, local_ref[v, p] - coef_ref[p] * rest)
    width = PLANES * VARS
    copies = [
        pltpu.make_async_copy(src.at[:, 0:width], out_ref.at[:, SOURCE:TERM], sems.at[0]),
        pltpu.make_async_copy(src.at[:, width:], out_ref.at[:, TERM:], sems.at[1]),
    ]
    copies[0].start()
    for v in range(VARS):
        ring[v, 0:height] = pick(tile, v)
        ring[v, height : 2 * height] = pick(lax.rem(tile + 1, 4), v)
    for v in range(VARS):
        here = ring[v, pl.ds(offset, height)]
        after = ring[v, pl.ds(offset + 1, height)]
        put(width + v, (1.0 - weight) * here + weight * after)
    copies[1].start()
    for copy in copies:
        copy.wait()


def sweep_kernel(in_ref, out_ref):
    blocks = in_ref.shape[0]

    def block_of(b, p):
        base = p * COEFS
        s = [in_ref[b, base + a] for a in range(VARS)]
        k = {pair: in_ref[b, base + VARS + i] for i, pair in enumerate(PAIRS)}
        form = in_ref[b, FORM]
        return s, k, form == 0.0, form == 2.0

    def apply(block, x):
        s, k, is_row, is_col = block
        g = [jnp.where(is_col, s[b] * x[b], x[b]) for b in range(VARS)]
        out = []
        for a in range(VARS):
            terms = [k[a, b] * g[b] if a < b else k[b, a] * g[b] for b in range(VARS) if b != a]
            signs = [a < b for b in range(VARS) if b != a]
            plus = [t for t, up in zip(terms, signs) if up]
            minus = [t for t, up in zip(terms, signs) if not up]
            rest = tree(plus) - tree(minus) if plus and minus else (tree(plus) if plus else -tree(minus))
            out.append(s[a] * x[a] + jnp.where(is_row, s[a] * rest, rest))
        return out

    def tree(terms):
        while len(terms) > 1:
            terms = [sum(terms[i : i + 2][1:], terms[i]) for i in range(0, len(terms), 2)]
        return terms[0]

    def lower(b, x):
        before = lax.rem(b + blocks - 1, blocks)
        for p in range(PLANES):
            given = [in_ref[b, SOURCE + p * VARS + v] for v in range(VARS)]
            if p == 0:
                given = [given[v] + in_ref[before, TERM + v] for v in range(VARS)]
            x = apply(block_of(b, p), [given[v] + x[v] for v in range(VARS)])
            for v in range(VARS):
                out_ref[b, v * PLANES + p] = x[v]
        return x

    def upper(i, x):
        b = blocks - 1 - i
        for p in reversed(range(PLANES)):
            y = apply(block_of(b, p), x)
            x = [out_ref[b, v * PLANES + p] + y[v] for v in range(VARS)]
            for v in range(VARS):
                out_ref[b, v * PLANES + p] = x[v]
        return x

    zero = [jnp.zeros((PART, LANES), jnp.float32) for _ in range(VARS)]
    lax.fori_loop(0, blocks, lower, zero, unroll=2)
    lax.fori_loop(0, blocks, upper, zero, unroll=2)


def unpack_kernel(in_ref, out_ref):
    for v in range(VARS):
        for p in range(PLANES):
            for t in range(in_ref.shape[0]):
                out_ref[v, p, PART * t : PART * t + PART] = in_ref[t, v * PLANES + p]


def on_device(residual, dq_old, lateral_coef, diag_inverse, match_list, slide_weight):
    height = residual.shape[2]
    blocks = lax.axis_size("stream")
    f32 = jnp.float32
    grant = pltpu.CompilerParams(vmem_limit_bytes=24 * 1024 * 1024)
    rows = pl.pallas_call(
        edges_kernel,
        out_shape=jax.ShapeDtypeStruct((VARS * height + EDGE_ROWS, LANES), f32),
        in_specs=[vmem()],
        out_specs=vmem(),
        compiler_params=grant,
        name="edges",
    )(dq_old)
    cols = pl.pallas_call(
        columns_kernel,
        out_shape=jax.ShapeDtypeStruct((16, height), f32),
        in_specs=[vmem()],
        out_specs=vmem(),
        compiler_params=grant,
        name="columns",
    )(dq_old)
    far = lax.ppermute(rows, "passage", [(q, q ^ 2) for q in range(4)])
    cols = lax.ppermute(cols, "span", [(0, 1), (1, 0)])
    steps = 4
    packed = pl.pallas_call(
        pack_kernel,
        out_shape=jax.ShapeDtypeStruct((blocks, SENT, PART, LANES), f32),
        grid=(steps,),
        in_specs=[
            pl.BlockSpec((VARS, VARS, PLANES, height // steps, LANES), lambda i: (0, 0, 0, i, 0))
        ],
        out_specs=pl.BlockSpec((blocks // steps, SOURCE, PART, LANES), lambda i: (i, 0, 0, 0)),
        compiler_params=grant,
        name="pack",
    )(diag_inverse)
    core = lax.ppermute(rows, "passage", [(q, q ^ 1) for q in range(4)])
    local = pl.pallas_call(
        local_kernel,
        out_shape=jax.ShapeDtypeStruct((VARS, PLANES, height, LANES), f32),
        in_specs=[vmem()] * 4,
        out_specs=vmem(),
        compiler_params=grant,
        name="local",
    )(dq_old, residual, lateral_coef, core)
    cross = lax.ppermute(far, "passage", [(q, q ^ 1) for q in range(4)])
    any_space = pl.BlockSpec(memory_space=pl.ANY)
    sent = pl.pallas_call(
        source_kernel,
        out_shape=jax.ShapeDtypeStruct((blocks, SENT, PART, LANES), f32),
        in_specs=[pl.BlockSpec(memory_space=pltpu.SMEM)] + [vmem()] * 8 + [any_space],
        out_specs=any_space,
        scratch_shapes=[
            pltpu.VMEM((blocks, PLANES * VARS + VARS, PART, LANES), f32),
            pltpu.VMEM((VARS, 2 * height + 8, LANES), f32),
            pltpu.SemaphoreType.DMA((2,)),
        ],
        input_output_aliases={9: 0},
        compiler_params=grant,
        name="source",
    )(match_list, dq_old, local, lateral_coef, slide_weight[None], core, far, cross, cols, packed)
    got = lax.all_to_all(sent, "stream", 0, 0)
    swept = pl.pallas_call(
        sweep_kernel,
        out_shape=jax.ShapeDtypeStruct((blocks, PLANES * VARS, PART, LANES), f32),
        in_specs=[vmem()],
        out_specs=vmem(),
        compiler_params=grant,
        name="sweep",
    )(got)
    back = lax.all_to_all(swept, "stream", 0, 0)
    return pl.pallas_call(
        unpack_kernel,
        out_shape=jax.ShapeDtypeStruct((VARS, PLANES, height, LANES), f32),
        in_specs=[vmem()],
        out_specs=vmem(),
        compiler_params=grant,
        name="unpack",
    )(back)


def solution(mesh):
    placed = (
        P(None, "stream", "passage", "span"),
        P(None, "stream", "passage", "span"),
        P("stream", "passage", "span"),
        P(None, None, "stream", "passage", "span"),
        P("stream", "passage"),
        P("passage"),
    )
    return jax.shard_map(
        on_device,
        mesh=mesh,
        in_specs=placed,
        out_specs=P(None, "stream", "passage", "span"),
        check_vma=False,
    )
```

profile of v0, /device:TPU:0, one launch (start us, length us, event | category | flops | bytes accessed | tf_op | source)
XLA Modules:
  0.0 65.4 jit_solution(18334891991119817979)
XLA Ops:
  0.0 0.0 copy-start
  0.0 1.0 %copy-done = f32[6,2,64,128]{3,2,1,0:T(8,128)S(1)} copy-done((f32[6,2,64,128]{3,2,1,0:T(8,128)S(1)}, f32[6,2,64,128]{3,2,1,0:T(8,128)}, u32[]{:S(2)}) %copy-start) | copy-done | bytes 393240
  1.0 3.2 %collective-permute-start.1 = (f32[400,128]{1,0:T(8,128)S(1)}, f32[400,128]{1,0:T(8,128)S(1)}, u32[]{:S(2)}, u32[]{:S(2)}) collective-permute-start(f32[400,128]{1,0:T(8,128)S(1)} %edges.1), channel_id=1, source_target_pairs={{0,4},{2,6},{4,0},{6,2},{1,5},{3,7},{5,1},{7,3},{8,12},{10,14},{12... | collective-permute-start | bytes 614408 | tf_op jit(solution)/shard_map/ppermute | solution.py:238
  4.2 0.0 collective-permute-start
  4.2 5.1 %collective-permute-done.1.far_ref = f32[400,128]{1,0:T(8,128)S(1)} collective-permute-done((f32[400,128]{1,0:T(8,128)S(1)}, f32[400,128]{1,0:T(8,128)S(1)}, u32[]{:S(2)}, u32[]{:S(2)}) %collective-permute-start.1) | collective-permute-done | bytes 204832 | tf_op jit(solution)/shard_map/ppermute | solution.py:238
  9.3 0.0 collective-permute-start.2
  9.3 0.2 columns.1
  9.5 1.8 %collective-permute-start.3 = (f32[16,64]{1,0:T(8,128)S(1)}, f32[16,64]{1,0:T(8,128)S(1)}, u32[]{:S(2)}, u32[]{:S(2)}) collective-permute-start(f32[16,64]{1,0:T(8,128)S(1)} %columns.1), channel_id=1, source_target_pairs={{0,1},{1,0},{2,3},{3,2},{4,5},{5,4},{6,7},{7,6},{8,9},{9,8},{10,11... | collective-permute-start | bytes 12296 | tf_op jit(solution)/shard_map/ppermute | solution.py:239
  11.3 1.7 %copy-done.2 = f32[6,6,2,64,128]{4,3,2,1,0:T(8,128)S(1)} copy-done((f32[6,6,2,64,128]{4,3,2,1,0:T(8,128)S(1)}, f32[6,6,2,64,128]{4,3,2,1,0:T(8,128)}, u32[]{:S(2)}) %copy-start.2) | copy-done | bytes 2359320
  13.0 1.1 %pack.1._ = f32[16,61,4,128]{3,2,1,0:T(4,128)S(1)} custom-call(f32[6,6,2,64,128]{4,3,2,1,0:T(8,128)S(1)} %copy-done.2), custom_call_target="tpu_custom_call" | custom-call | tf_op jit(solution)/shard_map/pack/pallas_call | solution.py:241
  14.1 0.0 collective-permute-done.core_ref
  14.1 0.0 copy-done.1
  14.1 0.0 copy-done.3
  14.2 0.0 copy-done.4
  14.2 0.3 local.1.local_ref
  14.4 0.0 collective-permute-done.3.cols_ref
  14.5 0.0 collective-permute-done.2.cross_ref
  14.5 0.0 copy-done.5
  14.5 0.0 copy-done.6
  14.5 0.9 %source.1 = f32[16,61,4,128]{3,2,1,0:T(4,128)S(1)} custom-call(s32[1,64]{1,0:T(1,128)S(1)} %copy-done.5, f32[6,2,64,128]{3,2,1,0:T(8,128)S(1)} %copy-done.1, f32[6,2,64,128]{3,2,1,0:T(8,128)S(1)} %local.1.local_ref, f32[2,64,128]{2,1,0:T(8,128)S(1)} %copy-done.4, f32[1,64]{1,0:T(1,128)S(1)} %bitcast.1, ...), custom_call_target="tpu_custom_call", output_to_operand_aliasing={{}: (9, {})} | custom-call | tf_op jit(solution)/shard_map/source/pallas_call | solution.py:263
  15.4 35.6 %all_to_all.10.in_ref = f32[16,61,4,128]{3,2,1,0:T(4,128)S(1)} all-to-all(f32[16,61,4,128]{3,2,1,0:T(4,128)S(1)} %source.1), channel_id=1, replica_groups=mesh['stream'=16,'passage'=4,'span'=2] {'stream'}, dimensions={0} | all-to-all | bytes 3997696 | tf_op jit(solution)/shard_map/all_to_all | solution.py:277
  51.0 0.9 %sweep.1 = f32[16,12,4,128]{3,2,1,0:T(4,128)S(1)} custom-call(f32[16,61,4,128]{3,2,1,0:T(4,128)S(1)} %all_to_all.10.in_ref), custom_call_target="tpu_custom_call" | custom-call | tf_op jit(solution)/shard_map/sweep/pallas_call | solution.py:278
  52.0 12.6 %all_to_all.11.in_ref = f32[16,12,4,128]{3,2,1,0:T(4,128)S(1)} all-to-all(f32[16,12,4,128]{3,2,1,0:T(4,128)S(1)} %sweep.1), channel_id=1, replica_groups=mesh['stream'=16,'passage'=4,'span'=2] {'stream'}, dimensions={0} | all-to-all | bytes 786432 | tf_op jit(solution)/shard_map/all_to_all | solution.py:286
  64.5 0.8 %unpack.1 = f32[6,2,64,128]{3,2,1,0:T(8,128)} custom-call(f32[16,12,4,128]{3,2,1,0:T(4,128)S(1)} %all_to_all.11.in_ref), custom_call_target="tpu_custom_call" | custom-call | tf_op jit(solution)/shard_map/unpack/pallas_call | solution.py:287
  (7 shorter events, 0.0 us)
Async XLA Ops:
  0.0 1.0 %copy-start = (f32[6,2,64,128]{3,2,1,0:T(8,128)S(1)}, f32[6,2,64,128]{3,2,1,0:T(8,128)}, u32[]{:S(2)}) copy-start(f32[6,2,64,128]{3,2,1,0:T(8,128)} %dq_ref.7) | copy-start | bytes 1179652
  1.0 8.3 %collective-permute-start.1 = (f32[400,128]{1,0:T(8,128)S(1)}, f32[400,128]{1,0:T(8,128)S(1)}, u32[]{:S(2)}, u32[]{:S(2)}) collective-permute-start(f32[400,128]{1,0:T(8,128)S(1)} %edges.1), channel_id=1, source_target_pairs={{0,4},{2,6},{4,0},{6,2},{1,5},{3,7},{5,1},{7,3},{8,12},{10,14},{12... | collective-permute-start | bytes 614408 | tf_op jit(solution)/shard_map/ppermute | solution.py:238
  4.2 9.9 %collective-permute-start = (f32[400,128]{1,0:T(8,128)S(1)}, f32[400,128]{1,0:T(8,128)S(1)}, u32[]{:S(2)}, u32[]{:S(2)}) collective-permute-start(f32[400,128]{1,0:T(8,128)S(1)} %edges.1), channel_id=1, source_target_pairs={{0,2},{2,0},{4,6},{6,4},{1,3},{3,1},{5,7},{7,5},{8,10},{10,8},{12,... | collective-permute-start | bytes 614408 | tf_op jit(solution)/shard_map/ppermute | solution.py:252
  9.3 5.1 %collective-permute-start.2 = (f32[400,128]{1,0:T(8,128)S(1)}, f32[400,128]{1,0:T(8,128)S(1)}, u32[]{:S(2)}, u32[]{:S(2)}) collective-permute-start(f32[400,128]{1,0:T(8,128)S(1)} %collective-permute-done.1.far_ref), channel_id=1, source_target_pairs={{0,2},{2,0},{4,6},{6,4},{1,3},{3,1},{5,7},{7,5},{8,10},{10,8},{12,... | collective-permute-start | bytes 614408 | tf_op jit(solution)/shard_map/ppermute | solution.py:261
  9.5 4.6 %copy-start.1 = (f32[6,2,64,128]{3,2,1,0:T(8,128)S(1)}, f32[6,2,64,128]{3,2,1,0:T(8,128)}, u32[]{:S(2)}) copy-start(f32[6,2,64,128]{3,2,1,0:T(8,128)} %dq_ref.7) | copy-start | bytes 1179652
  9.5 4.9 %collective-permute-start.3 = (f32[16,64]{1,0:T(8,128)S(1)}, f32[16,64]{1,0:T(8,128)S(1)}, u32[]{:S(2)}, u32[]{:S(2)}) collective-permute-start(f32[16,64]{1,0:T(8,128)S(1)} %columns.1), channel_id=1, source_target_pairs={{0,1},{1,0},{2,3},{3,2},{4,5},{5,4},{6,7},{7,6},{8,9},{9,8},{10,11... | collective-permute-start | bytes 12296 | tf_op jit(solution)/shard_map/ppermute | solution.py:239
  11.3 1.7 %copy-start.2 = (f32[6,6,2,64,128]{4,3,2,1,0:T(8,128)S(1)}, f32[6,6,2,64,128]{4,3,2,1,0:T(8,128)}, u32[]{:S(2)}) copy-start(f32[6,6,2,64,128]{4,3,2,1,0:T(8,128)} %d_ref.1) | copy-start | bytes 7077892
  13.0 1.2 %copy-start.3 = (f32[6,2,64,128]{3,2,1,0:T(8,128)S(1)}, f32[6,2,64,128]{3,2,1,0:T(8,128)}, u32[]{:S(2)}) copy-start(f32[6,2,64,128]{3,2,1,0:T(8,128)} %res_ref.1) | copy-start | bytes 1179652
  13.0 1.2 %copy-start.4 = (f32[2,64,128]{2,1,0:T(8,128)S(1)}, f32[2,64,128]{2,1,0:T(8,128)}, u32[]{:S(2)}) copy-start(f32[2,64,128]{2,1,0:T(8,128)} %coef_ref.3) | copy-start | bytes 196612
  13.0 1.5 %copy-start.5 = (s32[1,64]{1,0:T(1,128)S(1)}, s32[1,64]{1,0:T(1,128)}, u32[]{:S(2)}) copy-start(s32[1,64]{1,0:T(1,128)} %match_ref.1) | copy-start | bytes 772
  13.0 1.5 %copy-start.6 = (f32[64]{0:T(128)S(1)}, f32[64]{0:T(128)}, u32[]{:S(2)}) copy-start(f32[64]{0:T(128)} %param.11) | copy-start | bytes 772
where the time goes:
time: 65.6 us; the launch traced here: 65.4 us
  blocking collectives  48.2 us (73%)
  waiting for transfers between devices  5.08 us (8%)
  starting transfers between devices  4.98 us (8%)
  Pallas kernels  4.36 us (7%)
  local copies, waits for them, and re-layouts  2.68 us (4%)
    all_to_all x1, blocking collectives, on_device(): got = lax.all_to_all(sent, 'stream', 0, 0)  35.6 us
    all_to_all x1, blocking collectives, on_device(): back = lax.all_to_all(swept, 'stream', 0, 0)  12.6 us
    ppermute x1, waiting for transfers between devices, on_device(): far = lax.ppermute(rows, 'passage', [(q, q ^ 2) for q in range(4)])  5.07 us
    ppermute x1, starting transfers between devices, on_device(): far = lax.ppermute(rows, 'passage', [(q, q ^ 2) for q in range(4)])  3.21 us
    unnamed x14, local copies, waits for them, and re-layouts  2.68 us
    ppermute x1, starting transfers between devices, on_device(): cols = lax.ppermute(cols, 'span', [(0, 1), (1, 0)])  1.76 us
  transfers between devices with their start and end apart: 4, of which 1 were waited for; matrix products, arithmetic and copies ran while one was open for 0% of the time, Pallas kernels for 3%

commit v1 on v0

--- a/solution.py
+++ b/solution.py
@@ -103,7 +103,7 @@
 
 
 def source_kernel(
-    match_ref, dq_ref, local_ref, coef_ref, weight_ref, core_ref, far_ref, cross_ref, cols_ref, _, out_ref, src, ring, sems
+    match_ref, dq_ref, local_ref, coef_ref, weight_ref, core_ref, far_ref, cross_ref, cols_ref, _, out_ref, ring
 ):
     q, span = lax.axis_index("passage"), lax.axis_index("span")
     height = dq_ref.shape[2]
@@ -126,7 +126,7 @@
 
     def put(index, value):
         for t in range(height // PART):
-            src[t, index] = value[PART * t : PART * t + PART]
+            out_ref[t, index] = value[PART * t : PART * t + PART]
 
     for v in range(VARS):
         for p in range(PLANES):
@@ -135,23 +135,14 @@
             i = v * PLANES + p
             side = pltpu.roll(cols, LANES - 1 - i, 1)
             rest = jnp.where(beyond, row, 0.0) + jnp.where(edge, side, 0.0)
-            put(p * VARS + v, local_ref[v, p] - coef_ref[p] * rest)
-    width = PLANES * VARS
-    copies = [
-        pltpu.make_async_copy(src.at[:, 0:width], out_ref.at[:, SOURCE:TERM], sems.at[0]),
-        pltpu.make_async_copy(src.at[:, width:], out_ref.at[:, TERM:], sems.at[1]),
-    ]
-    copies[0].start()
+            put(SOURCE + p * VARS + v, local_ref[v, p] - coef_ref[p] * rest)
     for v in range(VARS):
         ring[v, 0:height] = pick(tile, v)
         ring[v, height : 2 * height] = pick(lax.rem(tile + 1, 4), v)
     for v in range(VARS):
         here = ring[v, pl.ds(offset, height)]
         after = ring[v, pl.ds(offset + 1, height)]
-        put(width + v, (1.0 - weight) * here + weight * after)
-    copies[1].start()
-    for copy in copies:
-        copy.wait()
+        put(TERM + v, (1.0 - weight) * here + weight * after)
 
 
 def sweep_kernel(in_ref, out_ref):
@@ -162,25 +153,26 @@
         s = [in_ref[b, base + a] for a in range(VARS)]
         k = {pair: in_ref[b, base + VARS + i] for i, pair in enumerate(PAIRS)}
         form = in_ref[b, FORM]
-        return s, k, form == 0.0, form == 2.0
+        is_row, is_col = form == 0.0, form == 2.0
+        rows = [jnp.where(is_row, x, 1.0) for x in s]
+        columns = [jnp.where(is_col, x, 1.0) for x in s]
+        return s, k, rows, columns
 
     def apply(block, x):
-        s, k, is_row, is_col = block
-        g = [jnp.where(is_col, s[b] * x[b], x[b]) for b in range(VARS)]
+        s, k, rows, columns = block
+        g = [columns[b] * x[b] for b in range(VARS)]
         out = []
         for a in range(VARS):
-            terms = [k[a, b] * g[b] if a < b else k[b, a] * g[b] for b in range(VARS) if b != a]
-            signs = [a < b for b in range(VARS) if b != a]
-            plus = [t for t, up in zip(terms, signs) if up]
-            minus = [t for t, up in zip(terms, signs) if not up]
-            rest = tree(plus) - tree(minus) if plus and minus else (tree(plus) if plus else -tree(minus))
-            out.append(s[a] * x[a] + jnp.where(is_row, s[a] * rest, rest))
+            plus = tree([k[a, b] * g[b] for b in range(a + 1, VARS)])
+            minus = tree([k[b, a] * g[b] for b in range(a)])
+            rest = minus if plus is None else plus if minus is None else plus - minus
+            out.append(s[a] * x[a] + rows[a] * (-rest if plus is None else rest))
         return out
 
     def tree(terms):
         while len(terms) > 1:
             terms = [sum(terms[i : i + 2][1:], terms[i]) for i in range(0, len(terms), 2)]
-        return terms[0]
+        return terms[0] if terms else None
 
     def lower(b, x):
         before = lax.rem(b + blocks - 1, blocks)
@@ -203,15 +195,20 @@
         return x
 
     zero = [jnp.zeros((PART, LANES), jnp.float32) for _ in range(VARS)]
-    lax.fori_loop(0, blocks, lower, zero, unroll=2)
-    lax.fori_loop(0, blocks, upper, zero, unroll=2)
-
-
-def unpack_kernel(in_ref, out_ref):
+    lax.fori_loop(0, blocks, lower, zero, unroll=16)
+    lax.fori_loop(0, blocks, upper, zero, unroll=16)
+
+
+def unpack_kernel(in_ref, out_ref, held, sems):
+    copies = []
     for v in range(VARS):
         for p in range(PLANES):
             for t in range(in_ref.shape[0]):
-                out_ref[v, p, PART * t : PART * t + PART] = in_ref[t, v * PLANES + p]
+                held[v, p, PART * t : PART * t + PART] = in_ref[t, v * PLANES + p]
+        copies.append(pltpu.make_async_copy(held.at[v], out_ref.at[v], sems.at[v]))
+        copies[v].start()
+    for copy in copies:
+        copy.wait()
 
 
 def on_device(residual, dq_old, lateral_coef, diag_inverse, match_list, slide_weight):
@@ -259,16 +256,13 @@
         name="local",
     )(dq_old, residual, lateral_coef, core)
     cross = lax.ppermute(far, "passage", [(q, q ^ 1) for q in range(4)])
-    any_space = pl.BlockSpec(memory_space=pl.ANY)
     sent = pl.pallas_call(
         source_kernel,
         out_shape=jax.ShapeDtypeStruct((blocks, SENT, PART, LANES), f32),
-        in_specs=[pl.BlockSpec(memory_space=pltpu.SMEM)] + [vmem()] * 8 + [any_space],
-        out_specs=any_space,
+        in_specs=[pl.BlockSpec(memory_space=pltpu.SMEM)] + [vmem()] * 9,
+        out_specs=vmem(),
         scratch_shapes=[
-            pltpu.VMEM((blocks, PLANES * VARS + VARS, PART, LANES), f32),
             pltpu.VMEM((VARS, 2 * height + 8, LANES), f32),
-            pltpu.SemaphoreType.DMA((2,)),
         ],
         input_output_aliases={9: 0},
         compiler_params=grant,
@@ -288,7 +282,11 @@
         unpack_kernel,
         out_shape=jax.ShapeDtypeStruct((VARS, PLANES, height, LANES), f32),
         in_specs=[vmem()],
-        out_specs=vmem(),
+        out_specs=pl.BlockSpec(memory_space=pltpu.HBM),
+        scratch_shapes=[
+            pltpu.VMEM((VARS, PLANES, height, LANES), f32),
+            pltpu.SemaphoreType.DMA((VARS,)),
+        ],
         compiler_params=grant,
         name="unpack",
     )(back)

time: 65.6 us -> 65.3 us (level)
  no operation moved by 1% of the time
where the time goes in v1:
time: 65.3 us; the launch traced here: 65.1 us
  blocking collectives  48.2 us (74%)
  waiting for transfers between devices  5.08 us (8%)
  starting transfers between devices  4.98 us (8%)
  Pallas kernels  4.1 us (6%)
  local copies, waits for them, and re-layouts  2.68 us (4%)
    all_to_all x1, blocking collectives, on_device(): got = lax.all_to_all(sent, 'stream', 0, 0)  35.6 us
    all_to_all x1, blocking collectives, on_device(): back = lax.all_to_all(swept, 'stream', 0, 0)  12.6 us
    ppermute x1, waiting for transfers between devices, on_device(): far = lax.ppermute(rows, 'passage', [(q, q ^ 2) for q in range(4)])  5.07 us
    ppermute x1, starting transfers between devices, on_device(): far = lax.ppermute(rows, 'passage', [(q, q ^ 2) for q in range(4)])  3.21 us
    unnamed x14, local copies, waits for them, and re-layouts  2.68 us
    ppermute x1, starting transfers between devices, on_device(): cols = lax.ppermute(cols, 'span', [(0, 1), (1, 0)])  1.76 us
  transfers between devices with their start and end apart: 4, of which 1 were waited for; matrix products, arithmetic and copies ran while one was open for 0% of the time, Pallas kernels for 3%

profile of v1, /device:TPU:0, one launch (start us, length us, event | category | flops | bytes accessed | tf_op | source)
XLA Modules:
  0.0 65.1 jit_solution(10645183541275968259)
XLA Ops:
  0.0 0.0 copy-start
  0.0 1.0 %copy-done = f32[6,2,64,128]{3,2,1,0:T(8,128)S(1)} copy-done((f32[6,2,64,128]{3,2,1,0:T(8,128)S(1)}, f32[6,2,64,128]{3,2,1,0:T(8,128)}, u32[]{:S(2)}) %copy-start) | copy-done | bytes 393240
  1.0 3.2 %collective-permute-start.1 = (f32[400,128]{1,0:T(8,128)S(1)}, f32[400,128]{1,0:T(8,128)S(1)}, u32[]{:S(2)}, u32[]{:S(2)}) collective-permute-start(f32[400,128]{1,0:T(8,128)S(1)} %edges.1), channel_id=1, source_target_pairs={{0,4},{2,6},{4,0},{6,2},{1,5},{3,7},{5,1},{7,3},{8,12},{10,14},{12... | collective-permute-start | bytes 614408 | tf_op jit(solution)/shard_map/ppermute | solution.py:235
  4.2 0.0 collective-permute-start
  4.2 5.1 %collective-permute-done.1.far_ref = f32[400,128]{1,0:T(8,128)S(1)} collective-permute-done((f32[400,128]{1,0:T(8,128)S(1)}, f32[400,128]{1,0:T(8,128)S(1)}, u32[]{:S(2)}, u32[]{:S(2)}) %collective-permute-start.1) | collective-permute-done | bytes 204832 | tf_op jit(solution)/shard_map/ppermute | solution.py:235
  9.3 0.0 collective-permute-start.2
  9.3 0.2 columns.1
  9.5 1.8 %collective-permute-start.3 = (f32[16,64]{1,0:T(8,128)S(1)}, f32[16,64]{1,0:T(8,128)S(1)}, u32[]{:S(2)}, u32[]{:S(2)}) collective-permute-start(f32[16,64]{1,0:T(8,128)S(1)} %columns.1), channel_id=1, source_target_pairs={{0,1},{1,0},{2,3},{3,2},{4,5},{5,4},{6,7},{7,6},{8,9},{9,8},{10,11... | collective-permute-start | bytes 12296 | tf_op jit(solution)/shard_map/ppermute | solution.py:236
  11.3 1.7 %copy-done.2 = f32[6,6,2,64,128]{4,3,2,1,0:T(8,128)S(1)} copy-done((f32[6,6,2,64,128]{4,3,2,1,0:T(8,128)S(1)}, f32[6,6,2,64,128]{4,3,2,1,0:T(8,128)}, u32[]{:S(2)}) %copy-start.2) | copy-done | bytes 2359320
  13.0 1.1 %pack.1._ = f32[16,61,4,128]{3,2,1,0:T(4,128)S(1)} custom-call(f32[6,6,2,64,128]{4,3,2,1,0:T(8,128)S(1)} %copy-done.2), custom_call_target="tpu_custom_call" | custom-call | tf_op jit(solution)/shard_map/pack/pallas_call | solution.py:238
  14.1 0.0 collective-permute-done.core_ref
  14.1 0.0 copy-done.1
  14.1 0.0 copy-done.3
  14.2 0.0 copy-done.4
  14.2 0.3 local.1.local_ref
  14.4 0.0 collective-permute-done.3.cols_ref
  14.5 0.0 collective-permute-done.2.cross_ref
  14.5 0.0 copy-done.5
  14.5 0.0 copy-done.6
  14.5 0.8 %source.1 = f32[16,61,4,128]{3,2,1,0:T(4,128)S(1)} custom-call(s32[1,64]{1,0:T(1,128)S(1)} %copy-done.5, f32[6,2,64,128]{3,2,1,0:T(8,128)S(1)} %copy-done.1, f32[6,2,64,128]{3,2,1,0:T(8,128)S(1)} %local.1.local_ref, f32[2,64,128]{2,1,0:T(8,128)S(1)} %copy-done.4, f32[1,64]{1,0:T(1,128)S(1)} %bitcast.1, ...), custom_call_target="tpu_custom_call", output_to_operand_aliasing={{}: (9, {})} | custom-call | tf_op jit(solution)/shard_map/source/pallas_call | solution.py:259
  15.3 35.6 %all_to_all.10.in_ref = f32[16,61,4,128]{3,2,1,0:T(4,128)S(1)} all-to-all(f32[16,61,4,128]{3,2,1,0:T(4,128)S(1)} %source.1), channel_id=1, replica_groups=mesh['stream'=16,'passage'=4,'span'=2] {'stream'}, dimensions={0} | all-to-all | bytes 3997696 | tf_op jit(solution)/shard_map/all_to_all | solution.py:271
  50.9 0.8 %sweep.1 = f32[16,12,4,128]{3,2,1,0:T(4,128)S(1)} custom-call(f32[16,61,4,128]{3,2,1,0:T(4,128)S(1)} %all_to_all.10.in_ref), custom_call_target="tpu_custom_call" | custom-call | tf_op jit(solution)/shard_map/sweep/pallas_call | solution.py:272
  51.7 12.6 %all_to_all.11.in_ref = f32[16,12,4,128]{3,2,1,0:T(4,128)S(1)} all-to-all(f32[16,12,4,128]{3,2,1,0:T(4,128)S(1)} %sweep.1), channel_id=1, replica_groups=mesh['stream'=16,'passage'=4,'span'=2] {'stream'}, dimensions={0} | all-to-all | bytes 786432 | tf_op jit(solution)/shard_map/all_to_all | solution.py:280
  64.3 0.8 %unpack.1 = f32[6,2,64,128]{3,2,1,0:T(8,128)} custom-call(f32[16,12,4,128]{3,2,1,0:T(4,128)S(1)} %all_to_all.11.in_ref), custom_call_target="tpu_custom_call" | custom-call | tf_op jit(solution)/shard_map/unpack/pallas_call | solution.py:281
  (7 shorter events, 0.0 us)
Async XLA Ops:
  0.0 1.0 %copy-start = (f32[6,2,64,128]{3,2,1,0:T(8,128)S(1)}, f32[6,2,64,128]{3,2,1,0:T(8,128)}, u32[]{:S(2)}) copy-start(f32[6,2,64,128]{3,2,1,0:T(8,128)} %dq_ref.7) | copy-start | bytes 1179652
  1.0 8.3 %collective-permute-start.1 = (f32[400,128]{1,0:T(8,128)S(1)}, f32[400,128]{1,0:T(8,128)S(1)}, u32[]{:S(2)}, u32[]{:S(2)}) collective-permute-start(f32[400,128]{1,0:T(8,128)S(1)} %edges.1), channel_id=1, source_target_pairs={{0,4},{2,6},{4,0},{6,2},{1,5},{3,7},{5,1},{7,3},{8,12},{10,14},{12... | collective-permute-start | bytes 614408 | tf_op jit(solution)/shard_map/ppermute | solution.py:235
  4.2 9.9 %collective-permute-start = (f32[400,128]{1,0:T(8,128)S(1)}, f32[400,128]{1,0:T(8,128)S(1)}, u32[]{:S(2)}, u32[]{:S(2)}) collective-permute-start(f32[400,128]{1,0:T(8,128)S(1)} %edges.1), channel_id=1, source_target_pairs={{0,2},{2,0},{4,6},{6,4},{1,3},{3,1},{5,7},{7,5},{8,10},{10,8},{12,... | collective-permute-start | bytes 614408 | tf_op jit(solution)/shard_map/ppermute | solution.py:249
  9.3 5.1 %collective-permute-start.2 = (f32[400,128]{1,0:T(8,128)S(1)}, f32[400,128]{1,0:T(8,128)S(1)}, u32[]{:S(2)}, u32[]{:S(2)}) collective-permute-start(f32[400,128]{1,0:T(8,128)S(1)} %collective-permute-done.1.far_ref), channel_id=1, source_target_pairs={{0,2},{2,0},{4,6},{6,4},{1,3},{3,1},{5,7},{7,5},{8,10},{10,8},{12,... | collective-permute-start | bytes 614408 | tf_op jit(solution)/shard_map/ppermute | solution.py:258
  9.5 4.6 %copy-start.1 = (f32[6,2,64,128]{3,2,1,0:T(8,128)S(1)}, f32[6,2,64,128]{3,2,1,0:T(8,128)}, u32[]{:S(2)}) copy-start(f32[6,2,64,128]{3,2,1,0:T(8,128)} %dq_ref.7) | copy-start | bytes 1179652
  9.5 4.9 %collective-permute-start.3 = (f32[16,64]{1,0:T(8,128)S(1)}, f32[16,64]{1,0:T(8,128)S(1)}, u32[]{:S(2)}, u32[]{:S(2)}) collective-permute-start(f32[16,64]{1,0:T(8,128)S(1)} %columns.1), channel_id=1, source_target_pairs={{0,1},{1,0},{2,3},{3,2},{4,5},{5,4},{6,7},{7,6},{8,9},{9,8},{10,11... | collective-permute-start | bytes 12296 | tf_op jit(solution)/shard_map/ppermute | solution.py:236
  11.3 1.7 %copy-start.2 = (f32[6,6,2,64,128]{4,3,2,1,0:T(8,128)S(1)}, f32[6,6,2,64,128]{4,3,2,1,0:T(8,128)}, u32[]{:S(2)}) copy-start(f32[6,6,2,64,128]{4,3,2,1,0:T(8,128)} %d_ref.1) | copy-start | bytes 7077892
  13.0 1.2 %copy-start.3 = (f32[6,2,64,128]{3,2,1,0:T(8,128)S(1)}, f32[6,2,64,128]{3,2,1,0:T(8,128)}, u32[]{:S(2)}) copy-start(f32[6,2,64,128]{3,2,1,0:T(8,128)} %res_ref.1) | copy-start | bytes 1179652
  13.0 1.2 %copy-start.4 = (f32[2,64,128]{2,1,0:T(8,128)S(1)}, f32[2,64,128]{2,1,0:T(8,128)}, u32[]{:S(2)}) copy-start(f32[2,64,128]{2,1,0:T(8,128)} %coef_ref.3) | copy-start | bytes 196612
  13.0 1.5 %copy-start.5 = (s32[1,64]{1,0:T(1,128)S(1)}, s32[1,64]{1,0:T(1,128)}, u32[]{:S(2)}) copy-start(s32[1,64]{1,0:T(1,128)} %match_ref.1) | copy-start | bytes 772
  13.0 1.5 %copy-start.6 = (f32[64]{0:T(128)S(1)}, f32[64]{0:T(128)}, u32[]{:S(2)}) copy-start(f32[64]{0:T(128)} %param.11) | copy-start | bytes 772

commit v2 on v1

--- a/solution.py
+++ b/solution.py
@@ -102,47 +102,61 @@
     return height * VARS + 2 * v + 1, height * VARS + 2 * v
 
 
-def source_kernel(
-    match_ref, dq_ref, local_ref, coef_ref, weight_ref, core_ref, far_ref, cross_ref, cols_ref, _, out_ref, ring
+def donors_of(match_ref):
+    q = lax.axis_index("passage")
+    first = match_ref[...].astype(jnp.float32)[0:1, 0:1]
+    start = lax.rem(jnp.max(first).astype(jnp.int32) + 64, 256)
+    tile = start // 64
+    return jnp.bitwise_xor(tile, q), jnp.bitwise_xor(lax.rem(tile + 1, 4), q), lax.rem(start, 64)
+
+
+def middle_kernel(
+    match_ref, dq_ref, local_ref, coef_ref, weight_ref, core_ref, far_ref, cols_ref, _, out_ref, ring_ref, spread_ref
 ):
-    q, span = lax.axis_index("passage"), lax.axis_index("span")
+    span = lax.axis_index("span")
     height = dq_ref.shape[2]
-    start = lax.rem(match_ref[0, 0] + 64, 256)
-    tile, offset = start // 64, lax.rem(start, 64)
-    odd = lax.rem(q, 2) == 1
-    sub = lax.broadcasted_iota(jnp.int32, (height, LANES), 0)
     lane = lax.broadcasted_iota(jnp.int32, (height, LANES), 1)
-    beyond = sub == jnp.where(odd, height - 1, 0)
     edge = lane == jnp.where(span == 0, LANES - 1, 0)
-    weight = jnp.broadcast_to(weight_ref[...], (LANES, height)).T
+    spread_ref[...] = jnp.broadcast_to(weight_ref[...], (LANES, height)).T
     cols = jnp.concatenate([cols_ref[...], jnp.zeros((LANES - 16, height), jnp.float32)], 0).T
-
-    def pick(index, v):
-        way = jnp.bitwise_xor(index, q)
+    for v in range(VARS):
+        for p in range(PLANES):
+            side = pltpu.roll(cols, LANES - 1 - (v * PLANES + p), 1)
+            value = local_ref[v, p] - coef_ref[p] * jnp.where(edge, side, 0.0)
+            for t in range(height // PART):
+                out_ref[t, SOURCE + p * VARS + v] = value[PART * t : PART * t + PART]
+    ways = donors_of(match_ref)
+    for v in range(VARS):
         face = slice(height * v, height * (v + 1))
-        near = jnp.where(way == 0, dq_ref[v, 1], core_ref[face])
-        away = jnp.where(way == 2, far_ref[face], cross_ref[face])
-        return jnp.where(way < 2, near, away)
-
-    def put(index, value):
-        for t in range(height // PART):
-            out_ref[t, index] = value[PART * t : PART * t + PART]
-
-    for v in range(VARS):
+        for n in range(2):
+            near = jnp.where(ways[n] == 0, dq_ref[v, 1], core_ref[face])
+            ring_ref[v, height * n : height * (n + 1)] = jnp.where(ways[n] < 2, near, far_ref[face])
+
+
+def source_kernel(match_ref, coef_ref, cross_ref, near_ref, spread_ref, _, out_ref, ring):
+    height = coef_ref.shape[1]
+    odd = lax.rem(lax.axis_index("passage"), 2) == 1
+    sub = lax.broadcasted_iota(jnp.int32, (PART, LANES), 0)
+    beyond = sub == jnp.where(odd, PART - 1, 0)
+    part = jnp.where(odd, height // PART - 1, 0)
+    ways = donors_of(match_ref)
+    for v in range(VARS):
+        face = slice(height * v, height * (v + 1))
+        for n in range(2):
+            rows = slice(height * n, height * (n + 1))
+            ring[v, rows] = jnp.where(ways[n] == 3, cross_ref[face], near_ref[v, rows])
         for p in range(PLANES):
             last, first = edge_rows(v, p, height)
             row = jnp.where(odd, cross_ref[first : first + 1], cross_ref[last : last + 1])
-            i = v * PLANES + p
-            side = pltpu.roll(cols, LANES - 1 - i, 1)
-            rest = jnp.where(beyond, row, 0.0) + jnp.where(edge, side, 0.0)
-            put(SOURCE + p * VARS + v, local_ref[v, p] - coef_ref[p] * rest)
-    for v in range(VARS):
-        ring[v, 0:height] = pick(tile, v)
-        ring[v, height : 2 * height] = pick(lax.rem(tile + 1, 4), v)
-    for v in range(VARS):
-        here = ring[v, pl.ds(offset, height)]
-        after = ring[v, pl.ds(offset + 1, height)]
-        put(TERM + v, (1.0 - weight) * here + weight * after)
+            coef = jnp.where(odd, coef_ref[p, height - PART :], coef_ref[p, 0:PART])
+            index = SOURCE + p * VARS + v
+            out_ref[part, index] = out_ref[part, index] - coef * jnp.where(beyond, row, 0.0)
+    for v in range(VARS):
+        here = ring[v, pl.ds(ways[2], height)]
+        after = ring[v, pl.ds(ways[2] + 1, height)]
+        term = (1.0 - spread_ref[...]) * here + spread_ref[...] * after
+        for t in range(height // PART):
+            out_ref[t, TERM + v] = term[PART * t : PART * t + PART]
 
 
 def sweep_kernel(in_ref, out_ref):
@@ -256,18 +270,30 @@
         name="local",
     )(dq_old, residual, lateral_coef, core)
     cross = lax.ppermute(far, "passage", [(q, q ^ 1) for q in range(4)])
+    whole = jax.ShapeDtypeStruct((blocks, SENT, PART, LANES), f32)
+    sent, near, spread = pl.pallas_call(
+        middle_kernel,
+        out_shape=(
+            whole,
+            jax.ShapeDtypeStruct((VARS, 2 * height, LANES), f32),
+            jax.ShapeDtypeStruct((height, LANES), f32),
+        ),
+        in_specs=[vmem()] * 9,
+        out_specs=(vmem(), vmem(), vmem()),
+        input_output_aliases={8: 0},
+        compiler_params=grant,
+        name="middle",
+    )(match_list, dq_old, local, lateral_coef, slide_weight[None], core, far, cols, packed)
     sent = pl.pallas_call(
         source_kernel,
-        out_shape=jax.ShapeDtypeStruct((blocks, SENT, PART, LANES), f32),
-        in_specs=[pl.BlockSpec(memory_space=pltpu.SMEM)] + [vmem()] * 9,
-        out_specs=vmem(),
-        scratch_shapes=[
-            pltpu.VMEM((VARS, 2 * height + 8, LANES), f32),
-        ],
-        input_output_aliases={9: 0},
+        out_shape=whole,
+        in_specs=[vmem()] * 6,
+        out_specs=vmem(),
+        scratch_shapes=[pltpu.VMEM((VARS, 2 * height + 8, LANES), f32)],
+        input_output_aliases={5: 0},
         compiler_params=grant,
         name="source",
-    )(match_list, dq_old, local, lateral_coef, slide_weight[None], core, far, cross, cols, packed)
+    )(match_list, lateral_coef, cross, near, spread, sent)
     got = lax.all_to_all(sent, "stream", 0, 0)
     swept = pl.pallas_call(
         sweep_kernel,

time: 65.3 us -> 64.9 us (level)
  no operation moved by 1% of the time
where the time goes in v2:
time: 64.9 us; the launch traced here: 64.7 us
  blocking collectives  48.2 us (74%)
  waiting for transfers between devices  5.08 us (8%)
  starting transfers between devices  4.98 us (8%)
  Pallas kernels  3.67 us (6%)
  local copies, waits for them, and re-layouts  2.68 us (4%)
    all_to_all x1, blocking collectives, on_device(): got = lax.all_to_all(sent, 'stream', 0, 0)  35.6 us
    all_to_all x1, blocking collectives, on_device(): back = lax.all_to_all(swept, 'stream', 0, 0)  12.6 us
    ppermute x1, waiting for transfers between devices, on_device(): far = lax.ppermute(rows, 'passage', [(q, q ^ 2) for q in range(4)])  5.07 us
    ppermute x1, starting transfers between devices, on_device(): far = lax.ppermute(rows, 'passage', [(q, q ^ 2) for q in range(4)])  3.21 us
    unnamed x14, local copies, waits for them, and re-layouts  2.68 us
    ppermute x1, starting transfers between devices, on_device(): cols = lax.ppermute(cols, 'span', [(0, 1), (1, 0)])  1.76 us
  transfers between devices with their start and end apart: 4, of which 1 were waited for; matrix products, arithmetic and copies ran while one was open for 0% of the time, Pallas kernels for 3%

profile of v2, /device:TPU:0, one launch (start us, length us, event | category | flops | bytes accessed | tf_op | source)
XLA Modules:
  0.0 64.7 jit_solution(11627464436396469859)
XLA Ops:
  0.0 1.0 %copy-done = f32[6,2,64,128]{3,2,1,0:T(8,128)S(1)} copy-done((f32[6,2,64,128]{3,2,1,0:T(8,128)S(1)}, f32[6,2,64,128]{3,2,1,0:T(8,128)}, u32[]{:S(2)}) %copy-start) | copy-done | bytes 393240
  1.0 3.2 %collective-permute-start = (f32[400,128]{1,0:T(8,128)S(1)}, f32[400,128]{1,0:T(8,128)S(1)}, u32[]{:S(2)}, u32[]{:S(2)}) collective-permute-start(f32[400,128]{1,0:T(8,128)S(1)} %edges.1), channel_id=1, source_target_pairs={{0,4},{2,6},{4,0},{6,2},{1,5},{3,7},{5,1},{7,3},{8,12},{10,14},{12... | collective-permute-start | bytes 614408 | tf_op jit(solution)/shard_map/ppermute | solution.py:249
  4.2 0.0 collective-permute-start.2
  4.2 5.1 %collective-permute-done.far_ref = f32[400,128]{1,0:T(8,128)S(1)} collective-permute-done((f32[400,128]{1,0:T(8,128)S(1)}, f32[400,128]{1,0:T(8,128)S(1)}, u32[]{:S(2)}, u32[]{:S(2)}) %collective-permute-start) | collective-permute-done | bytes 204832 | tf_op jit(solution)/shard_map/ppermute | solution.py:249
  9.3 0.0 collective-permute-start.1
  9.3 0.2 columns.1
  9.5 1.8 %collective-permute-start.3 = (f32[16,64]{1,0:T(8,128)S(1)}, f32[16,64]{1,0:T(8,128)S(1)}, u32[]{:S(2)}, u32[]{:S(2)}) collective-permute-start(f32[16,64]{1,0:T(8,128)S(1)} %columns.1), channel_id=1, source_target_pairs={{0,1},{1,0},{2,3},{3,2},{4,5},{5,4},{6,7},{7,6},{8,9},{9,8},{10,11... | collective-permute-start | bytes 12296 | tf_op jit(solution)/shard_map/ppermute | solution.py:250
  11.3 1.7 %copy-done.2 = f32[6,6,2,64,128]{4,3,2,1,0:T(8,128)S(1)} copy-done((f32[6,6,2,64,128]{4,3,2,1,0:T(8,128)S(1)}, f32[6,6,2,64,128]{4,3,2,1,0:T(8,128)}, u32[]{:S(2)}) %copy-start.2) | copy-done | bytes 2359320
  13.0 1.1 %pack.1._ = f32[16,61,4,128]{3,2,1,0:T(4,128)S(1)} custom-call(f32[6,6,2,64,128]{4,3,2,1,0:T(8,128)S(1)} %copy-done.2), custom_call_target="tpu_custom_call" | custom-call | tf_op jit(solution)/shard_map/pack/pallas_call | solution.py:252
  14.1 0.0 collective-permute-done.2.core_ref
  14.1 0.0 copy-done.1
  14.1 0.0 copy-done.3
  14.2 0.0 copy-done.4
  14.2 0.3 local.1.local_ref
  14.4 0.0 collective-permute-done.3.cols_ref
  14.5 0.0 copy-done.5
  14.5 0.0 copy-done.6
  14.5 0.3 middle.1
  14.7 0.0 collective-permute-done.1.cross_ref
  14.8 0.1 source.1
  14.9 35.6 %all_to_all.10.in_ref = f32[16,61,4,128]{3,2,1,0:T(4,128)S(1)} all-to-all(f32[16,61,4,128]{3,2,1,0:T(4,128)S(1)} %source.1), channel_id=1, replica_groups=mesh['stream'=16,'passage'=4,'span'=2] {'stream'}, dimensions={0} | all-to-all | bytes 3997696 | tf_op jit(solution)/shard_map/all_to_all | solution.py:297
  50.4 0.8 %sweep.1 = f32[16,12,4,128]{3,2,1,0:T(4,128)S(1)} custom-call(f32[16,61,4,128]{3,2,1,0:T(4,128)S(1)} %all_to_all.10.in_ref), custom_call_target="tpu_custom_call" | custom-call | tf_op jit(solution)/shard_map/sweep/pallas_call | solution.py:298
  51.3 12.6 %all_to_all.11.in_ref = f32[16,12,4,128]{3,2,1,0:T(4,128)S(1)} all-to-all(f32[16,12,4,128]{3,2,1,0:T(4,128)S(1)} %sweep.1), channel_id=1, replica_groups=mesh['stream'=16,'passage'=4,'span'=2] {'stream'}, dimensions={0} | all-to-all | bytes 786432 | tf_op jit(solution)/shard_map/all_to_all | solution.py:306
  63.9 0.8 %unpack.1 = f32[6,2,64,128]{3,2,1,0:T(8,128)} custom-call(f32[16,12,4,128]{3,2,1,0:T(4,128)S(1)} %all_to_all.11.in_ref), custom_call_target="tpu_custom_call" | custom-call | tf_op jit(solution)/shard_map/unpack/pallas_call | solution.py:307
  (8 shorter events, 0.0 us)
Async XLA Ops:
  0.0 1.0 %copy-start = (f32[6,2,64,128]{3,2,1,0:T(8,128)S(1)}, f32[6,2,64,128]{3,2,1,0:T(8,128)}, u32[]{:S(2)}) copy-start(f32[6,2,64,128]{3,2,1,0:T(8,128)} %dq_ref.7) | copy-start | bytes 1179652
  1.0 8.3 %collective-permute-start = (f32[400,128]{1,0:T(8,128)S(1)}, f32[400,128]{1,0:T(8,128)S(1)}, u32[]{:S(2)}, u32[]{:S(2)}) collective-permute-start(f32[400,128]{1,0:T(8,128)S(1)} %edges.1), channel_id=1, source_target_pairs={{0,4},{2,6},{4,0},{6,2},{1,5},{3,7},{5,1},{7,3},{8,12},{10,14},{12... | collective-permute-start | bytes 614408 | tf_op jit(solution)/shard_map/ppermute | solution.py:249
  4.2 9.9 %collective-permute-start.2 = (f32[400,128]{1,0:T(8,128)S(1)}, f32[400,128]{1,0:T(8,128)S(1)}, u32[]{:S(2)}, u32[]{:S(2)}) collective-permute-start(f32[400,128]{1,0:T(8,128)S(1)} %edges.1), channel_id=1, source_target_pairs={{0,2},{2,0},{4,6},{6,4},{1,3},{3,1},{5,7},{7,5},{8,10},{10,8},{12,... | collective-permute-start | bytes 614408 | tf_op jit(solution)/shard_map/ppermute | solution.py:263
  9.3 5.4 %collective-permute-start.1 = (f32[400,128]{1,0:T(8,128)S(1)}, f32[400,128]{1,0:T(8,128)S(1)}, u32[]{:S(2)}, u32[]{:S(2)}) collective-permute-start(f32[400,128]{1,0:T(8,128)S(1)} %collective-permute-done.far_ref), channel_id=1, source_target_pairs={{0,2},{2,0},{4,6},{6,4},{1,3},{3,1},{5,7},{7,5},{8,10},{10,8},{12,... | collective-permute-start | bytes 614408 | tf_op jit(solution)/shard_map/ppermute | solution.py:272
  9.5 4.6 %copy-start.1 = (f32[6,2,64,128]{3,2,1,0:T(8,128)S(1)}, f32[6,2,64,128]{3,2,1,0:T(8,128)}, u32[]{:S(2)}) copy-start(f32[6,2,64,128]{3,2,1,0:T(8,128)} %dq_ref.7) | copy-start | bytes 1179652
  9.5 4.9 %collective-permute-start.3 = (f32[16,64]{1,0:T(8,128)S(1)}, f32[16,64]{1,0:T(8,128)S(1)}, u32[]{:S(2)}, u32[]{:S(2)}) collective-permute-start(f32[16,64]{1,0:T(8,128)S(1)} %columns.1), channel_id=1, source_target_pairs={{0,1},{1,0},{2,3},{3,2},{4,5},{5,4},{6,7},{7,6},{8,9},{9,8},{10,11... | collective-permute-start | bytes 12296 | tf_op jit(solution)/shard_map/ppermute | solution.py:250
  11.3 1.7 %copy-start.2 = (f32[6,6,2,64,128]{4,3,2,1,0:T(8,128)S(1)}, f32[6,6,2,64,128]{4,3,2,1,0:T(8,128)}, u32[]{:S(2)}) copy-start(f32[6,6,2,64,128]{4,3,2,1,0:T(8,128)} %d_ref.1) | copy-start | bytes 7077892
  13.0 1.2 %copy-start.3 = (f32[2,64,128]{2,1,0:T(8,128)S(1)}, f32[2,64,128]{2,1,0:T(8,128)}, u32[]{:S(2)}) copy-start(f32[2,64,128]{2,1,0:T(8,128)} %coef_ref.5) | copy-start | bytes 196612
  13.0 1.2 %copy-start.4 = (f32[6,2,64,128]{3,2,1,0:T(8,128)S(1)}, f32[6,2,64,128]{3,2,1,0:T(8,128)}, u32[]{:S(2)}) copy-start(f32[6,2,64,128]{3,2,1,0:T(8,128)} %res_ref.1) | copy-start | bytes 1179652
  13.0 1.5 %copy-start.5 = (s32[1,64]{1,0:T(1,128)S(1)}, s32[1,64]{1,0:T(1,128)}, u32[]{:S(2)}) copy-start(s32[1,64]{1,0:T(1,128)} %match_ref.3) | copy-start | bytes 772
  13.0 1.5 %copy-start.6 = (f32[64]{0:T(128)S(1)}, f32[64]{0:T(128)}, u32[]{:S(2)}) copy-start(f32[64]{0:T(128)} %param.11) | copy-start | bytes 772

commit v3 on v2

--- a/solution.py
+++ b/solution.py
@@ -1,3 +1,5 @@
+import functools
+
 import jax
 import jax.numpy as jnp
 from jax import lax
@@ -166,21 +168,21 @@
         base = p * COEFS
         s = [in_ref[b, base + a] for a in range(VARS)]
         k = {pair: in_ref[b, base + VARS + i] for i, pair in enumerate(PAIRS)}
-        form = in_ref[b, FORM]
-        is_row, is_col = form == 0.0, form == 2.0
-        rows = [jnp.where(is_row, x, 1.0) for x in s]
-        columns = [jnp.where(is_col, x, 1.0) for x in s]
-        return s, k, rows, columns
-
-    def apply(block, x):
-        s, k, rows, columns = block
-        g = [columns[b] * x[b] for b in range(VARS)]
+        return s, k, in_ref[b, FORM]
+
+    def apply(block, x, general):
+        s, k, form = block
+        g = [jnp.where(form == 2.0, s[b], 1.0) * x[b] for b in range(VARS)] if general else x
         out = []
         for a in range(VARS):
             plus = tree([k[a, b] * g[b] for b in range(a + 1, VARS)])
             minus = tree([k[b, a] * g[b] for b in range(a)])
             rest = minus if plus is None else plus if minus is None else plus - minus
-            out.append(s[a] * x[a] + rows[a] * (-rest if plus is None else rest))
+            rest = -rest if plus is None else rest
+            if general:
+                out.append(s[a] * x[a] + jnp.where(form == 0.0, s[a], 1.0) * rest)
+            else:
+                out.append(s[a] * (x[a] + rest))
         return out
 
     def tree(terms):
@@ -188,29 +190,37 @@
             terms = [sum(terms[i : i + 2][1:], terms[i]) for i in range(0, len(terms), 2)]
         return terms[0] if terms else None
 
-    def lower(b, x):
+    def lower(general, b, x):
         before = lax.rem(b + blocks - 1, blocks)
         for p in range(PLANES):
             given = [in_ref[b, SOURCE + p * VARS + v] for v in range(VARS)]
             if p == 0:
                 given = [given[v] + in_ref[before, TERM + v] for v in range(VARS)]
-            x = apply(block_of(b, p), [given[v] + x[v] for v in range(VARS)])
+            x = apply(block_of(b, p), [given[v] + x[v] for v in range(VARS)], general)
             for v in range(VARS):
                 out_ref[b, v * PLANES + p] = x[v]
         return x
 
-    def upper(i, x):
+    def upper(general, i, x):
         b = blocks - 1 - i
         for p in reversed(range(PLANES)):
-            y = apply(block_of(b, p), x)
+            y = apply(block_of(b, p), x, general)
             x = [out_ref[b, v * PLANES + p] + y[v] for v in range(VARS)]
             for v in range(VARS):
                 out_ref[b, v * PLANES + p] = x[v]
         return x
 
-    zero = [jnp.zeros((PART, LANES), jnp.float32) for _ in range(VARS)]
-    lax.fori_loop(0, blocks, lower, zero, unroll=16)
-    lax.fori_loop(0, blocks, upper, zero, unroll=16)
+    def sweep(general):
+        zero = [jnp.zeros((PART, LANES), jnp.float32) for _ in range(VARS)]
+        lax.fori_loop(0, blocks, functools.partial(lower, general), zero, unroll=blocks)
+        lax.fori_loop(0, blocks, functools.partial(upper, general), zero, unroll=blocks)
+
+    form = in_ref[0, FORM]
+    for b in range(1, blocks):
+        form = jnp.maximum(form, in_ref[b, FORM])
+    scaled = jnp.max(form) == 0.0
+    pl.when(scaled)(lambda: sweep(False))
+    pl.when(jnp.logical_not(scaled))(lambda: sweep(True))
 
 
 def unpack_kernel(in_ref, out_ref, held, sems):
@@ -300,7 +310,7 @@
         out_shape=jax.ShapeDtypeStruct((blocks, PLANES * VARS, PART, LANES), f32),
         in_specs=[vmem()],
         out_specs=vmem(),
-        compiler_params=grant,
+        compiler_params=pltpu.CompilerParams(vmem_limit_bytes=24 * 1024 * 1024),
         name="sweep",
     )(got)
     back = lax.all_to_all(swept, "stream", 0, 0)

time: 64.9 us -> 64.9 us (level)
  no operation moved by 1% of the time
where the time goes in v3:
time: 64.9 us; the launch traced here: 64.6 us
  blocking collectives  48.2 us (74%)
  waiting for transfers between devices  5.08 us (8%)
  starting transfers between devices  4.98 us (8%)
  Pallas kernels  3.64 us (6%)
  local copies, waits for them, and re-layouts  2.68 us (4%)
    all_to_all x1, blocking collectives, on_device(): got = lax.all_to_all(sent, 'stream', 0, 0)  35.6 us
    all_to_all x1, blocking collectives, on_device(): back = lax.all_to_all(swept, 'stream', 0, 0)  12.6 us
    ppermute x1, waiting for transfers between devices, on_device(): far = lax.ppermute(rows, 'passage', [(q, q ^ 2) for q in range(4)])  5.07 us
    ppermute x1, starting transfers between devices, on_device(): far = lax.ppermute(rows, 'passage', [(q, q ^ 2) for q in range(4)])  3.21 us
    unnamed x14, local copies, waits for them, and re-layouts  2.68 us
    ppermute x1, starting transfers between devices, on_device(): cols = lax.ppermute(cols, 'span', [(0, 1), (1, 0)])  1.76 us
  transfers between devices with their start and end apart: 4, of which 1 were waited for; matrix products, arithmetic and copies ran while one was open for 0% of the time, Pallas kernels for 3%

profile of v3, /device:TPU:0, one launch (start us, length us, event | category | flops | bytes accessed | tf_op | source)
XLA Modules:
  0.0 64.6 jit_solution(11475567345989756042)
XLA Ops:
  0.0 1.0 %copy-done = f32[6,2,64,128]{3,2,1,0:T(8,128)S(1)} copy-done((f32[6,2,64,128]{3,2,1,0:T(8,128)S(1)}, f32[6,2,64,128]{3,2,1,0:T(8,128)}, u32[]{:S(2)}) %copy-start) | copy-done | bytes 393240
  1.0 3.2 %collective-permute-start = (f32[400,128]{1,0:T(8,128)S(1)}, f32[400,128]{1,0:T(8,128)S(1)}, u32[]{:S(2)}, u32[]{:S(2)}) collective-permute-start(f32[400,128]{1,0:T(8,128)S(1)} %edges.1), channel_id=1, source_target_pairs={{0,4},{2,6},{4,0},{6,2},{1,5},{3,7},{5,1},{7,3},{8,12},{10,14},{12... | collective-permute-start | bytes 614408 | tf_op jit(solution)/shard_map/ppermute | solution.py:259
  4.2 0.0 collective-permute-start.2
  4.2 5.1 %collective-permute-done.far_ref = f32[400,128]{1,0:T(8,128)S(1)} collective-permute-done((f32[400,128]{1,0:T(8,128)S(1)}, f32[400,128]{1,0:T(8,128)S(1)}, u32[]{:S(2)}, u32[]{:S(2)}) %collective-permute-start) | collective-permute-done | bytes 204832 | tf_op jit(solution)/shard_map/ppermute | solution.py:259
  9.3 0.0 collective-permute-start.1
  9.3 0.2 columns.1
  9.5 1.8 %collective-permute-start.3 = (f32[16,64]{1,0:T(8,128)S(1)}, f32[16,64]{1,0:T(8,128)S(1)}, u32[]{:S(2)}, u32[]{:S(2)}) collective-permute-start(f32[16,64]{1,0:T(8,128)S(1)} %columns.1), channel_id=1, source_target_pairs={{0,1},{1,0},{2,3},{3,2},{4,5},{5,4},{6,7},{7,6},{8,9},{9,8},{10,11... | collective-permute-start | bytes 12296 | tf_op jit(solution)/shard_map/ppermute | solution.py:260
  11.3 1.7 %copy-done.2 = f32[6,6,2,64,128]{4,3,2,1,0:T(8,128)S(1)} copy-done((f32[6,6,2,64,128]{4,3,2,1,0:T(8,128)S(1)}, f32[6,6,2,64,128]{4,3,2,1,0:T(8,128)}, u32[]{:S(2)}) %copy-start.2) | copy-done | bytes 2359320
  13.0 1.1 %pack.1._ = f32[16,61,4,128]{3,2,1,0:T(4,128)S(1)} custom-call(f32[6,6,2,64,128]{4,3,2,1,0:T(8,128)S(1)} %copy-done.2), custom_call_target="tpu_custom_call" | custom-call | tf_op jit(solution)/shard_map/pack/pallas_call | solution.py:262
  14.1 0.0 collective-permute-done.2.core_ref
  14.1 0.0 copy-done.1
  14.1 0.0 copy-done.3
  14.2 0.0 copy-done.4
  14.2 0.3 local.1.local_ref
  14.4 0.0 collective-permute-done.3.cols_ref
  14.5 0.0 copy-done.5
  14.5 0.0 copy-done.6
  14.5 0.3 middle.1
  14.7 0.0 collective-permute-done.1.cross_ref
  14.8 0.1 source.1
  14.9 35.6 %all_to_all.10.in_ref = f32[16,61,4,128]{3,2,1,0:T(4,128)S(1)} all-to-all(f32[16,61,4,128]{3,2,1,0:T(4,128)S(1)} %source.1), channel_id=1, replica_groups=mesh['stream'=16,'passage'=4,'span'=2] {'stream'}, dimensions={0} | all-to-all | bytes 3997696 | tf_op jit(solution)/shard_map/all_to_all | solution.py:307
  50.4 0.8 %sweep.1 = f32[16,12,4,128]{3,2,1,0:T(4,128)S(1)} custom-call(f32[16,61,4,128]{3,2,1,0:T(4,128)S(1)} %all_to_all.10.in_ref), custom_call_target="tpu_custom_call" | custom-call | tf_op jit(solution)/shard_map/sweep/pallas_call | solution.py:308
  51.3 12.6 %all_to_all.11.in_ref = f32[16,12,4,128]{3,2,1,0:T(4,128)S(1)} all-to-all(f32[16,12,4,128]{3,2,1,0:T(4,128)S(1)} %sweep.1), channel_id=1, replica_groups=mesh['stream'=16,'passage'=4,'span'=2] {'stream'}, dimensions={0} | all-to-all | bytes 786432 | tf_op jit(solution)/shard_map/all_to_all | solution.py:316
  63.8 0.8 %unpack.1 = f32[6,2,64,128]{3,2,1,0:T(8,128)} custom-call(f32[16,12,4,128]{3,2,1,0:T(4,128)S(1)} %all_to_all.11.in_ref), custom_call_target="tpu_custom_call" | custom-call | tf_op jit(solution)/shard_map/unpack/pallas_call | solution.py:317
  (8 shorter events, 0.0 us)
Async XLA Ops:
  0.0 1.0 %copy-start = (f32[6,2,64,128]{3,2,1,0:T(8,128)S(1)}, f32[6,2,64,128]{3,2,1,0:T(8,128)}, u32[]{:S(2)}) copy-start(f32[6,2,64,128]{3,2,1,0:T(8,128)} %dq_ref.7) | copy-start | bytes 1179652
  1.0 8.3 %collective-permute-start = (f32[400,128]{1,0:T(8,128)S(1)}, f32[400,128]{1,0:T(8,128)S(1)}, u32[]{:S(2)}, u32[]{:S(2)}) collective-permute-start(f32[400,128]{1,0:T(8,128)S(1)} %edges.1), channel_id=1, source_target_pairs={{0,4},{2,6},{4,0},{6,2},{1,5},{3,7},{5,1},{7,3},{8,12},{10,14},{12... | collective-permute-start | bytes 614408 | tf_op jit(solution)/shard_map/ppermute | solution.py:259
  4.2 9.9 %collective-permute-start.2 = (f32[400,128]{1,0:T(8,128)S(1)}, f32[400,128]{1,0:T(8,128)S(1)}, u32[]{:S(2)}, u32[]{:S(2)}) collective-permute-start(f32[400,128]{1,0:T(8,128)S(1)} %edges.1), channel_id=1, source_target_pairs={{0,2},{2,0},{4,6},{6,4},{1,3},{3,1},{5,7},{7,5},{8,10},{10,8},{12,... | collective-permute-start | bytes 614408 | tf_op jit(solution)/shard_map/ppermute | solution.py:273
  9.3 5.4 %collective-permute-start.1 = (f32[400,128]{1,0:T(8,128)S(1)}, f32[400,128]{1,0:T(8,128)S(1)}, u32[]{:S(2)}, u32[]{:S(2)}) collective-permute-start(f32[400,128]{1,0:T(8,128)S(1)} %collective-permute-done.far_ref), channel_id=1, source_target_pairs={{0,2},{2,0},{4,6},{6,4},{1,3},{3,1},{5,7},{7,5},{8,10},{10,8},{12,... | collective-permute-start | bytes 614408 | tf_op jit(solution)/shard_map/ppermute | solution.py:282
  9.5 4.6 %copy-start.1 = (f32[6,2,64,128]{3,2,1,0:T(8,128)S(1)}, f32[6,2,64,128]{3,2,1,0:T(8,128)}, u32[]{:S(2)}) copy-start(f32[6,2,64,128]{3,2,1,0:T(8,128)} %dq_ref.7) | copy-start | bytes 1179652
  9.5 4.9 %collective-permute-start.3 = (f32[16,64]{1,0:T(8,128)S(1)}, f32[16,64]{1,0:T(8,128)S(1)}, u32[]{:S(2)}, u32[]{:S(2)}) collective-permute-start(f32[16,64]{1,0:T(8,128)S(1)} %columns.1), channel_id=1, source_target_pairs={{0,1},{1,0},{2,3},{3,2},{4,5},{5,4},{6,7},{7,6},{8,9},{9,8},{10,11... | collective-permute-start | bytes 12296 | tf_op jit(solution)/shard_map/ppermute | solution.py:260
  11.3 1.7 %copy-start.2 = (f32[6,6,2,64,128]{4,3,2,1,0:T(8,128)S(1)}, f32[6,6,2,64,128]{4,3,2,1,0:T(8,128)}, u32[]{:S(2)}) copy-start(f32[6,6,2,64,128]{4,3,2,1,0:T(8,128)} %d_ref.1) | copy-start | bytes 7077892
  13.0 1.2 %copy-start.3 = (f32[2,64,128]{2,1,0:T(8,128)S(1)}, f32[2,64,128]{2,1,0:T(8,128)}, u32[]{:S(2)}) copy-start(f32[2,64,128]{2,1,0:T(8,128)} %coef_ref.5) | copy-start | bytes 196612
  13.0 1.2 %copy-start.4 = (f32[6,2,64,128]{3,2,1,0:T(8,128)S(1)}, f32[6,2,64,128]{3,2,1,0:T(8,128)}, u32[]{:S(2)}) copy-start(f32[6,2,64,128]{3,2,1,0:T(8,128)} %res_ref.1) | copy-start | bytes 1179652
  13.0 1.5 %copy-start.5 = (s32[1,64]{1,0:T(1,128)S(1)}, s32[1,64]{1,0:T(1,128)}, u32[]{:S(2)}) copy-start(s32[1,64]{1,0:T(1,128)} %match_ref.3) | copy-start | bytes 772
  13.0 1.5 %copy-start.6 = (f32[64]{0:T(128)S(1)}, f32[64]{0:T(128)}, u32[]{:S(2)}) copy-start(f32[64]{0:T(128)} %param.11) | copy-start | bytes 772
